TPU v7x, 32 devices: a whole 2x2x4 slice. The times are simulated.
32 devices in a mesh: blk: 16 (over z, x, core), tp: 2 (over y).
Axes of the slice: x: 2, y: 2, z: 4, core: 2. Of those that a mesh axis runs over, the one named last changes fastest.
Arguments:
- inputs: bfloat16 [2048, 8192], P('blk', 'tp'), may hold values from -6 to 6
- grad_out: bfloat16 [2048, 8192], P('blk', 'tp'), may hold values from -6 to 6
- w_up: bfloat16 [32, 2, 128, 128], P('blk'), may hold values from -0.4375 to 0.4375
- w_down: bfloat16 [32, 2, 128, 128], P('blk'), may hold values from -0.625 to 0.625
- up_rows: int32 [32, 2], P('blk'), may hold values from 0 to 63, as said below
- slot_counts: int32 [32], P('blk'), may hold values from 1 to 2
- keep_mask: int32 [2048, 256], P(None, 'blk'), may hold values from 0 to 65535, as said below
Outputs:
- outputs: bfloat16 [2048, 8192], P('blk', 'tp')
- grad_in: bfloat16 [2048, 8192], P('blk', 'tp')
- grad_up: bfloat16 [32, 2, 128, 128], P('blk', None, 'tp')
- grad_down: bfloat16 [32, 2, 128, 128], P('blk', None, 'tp')
Inputs may be any that keep to these rules, and one draw needn't show every extreme that they name: `up_rows`: within each hidden column block, the 2 entries are distinct. `keep_mask`: bit k of word w holds the keep flag of hidden unit 16 w + k.
All inputs are finite; a program needn't handle non-finite values.
Results may differ from a plain program's by a relative error of at most 0.005.
Values may be sent and summed in bfloat16 or wider, within the bound.
No kernel may reach another device: no remote copies, remote signals or barrier semaphores. Data moves between devices by JAX's collectives and lax.ppermute only.
A program may use at most 64 MiB of HBM per device.

v0:
```python
import jax
import jax.numpy as jnp
from jax import lax
from jax.sharding import PartitionSpec as P

INV_ROOT_TWO = 0.7071067811865476
INV_ROOT_TAU = 0.3989422804014327
KEEP_SCALE = 1.25


def gelu_value(value):
    return 0.5 * value * (1.0 + jax.scipy.special.erf(value * INV_ROOT_TWO))


def gelu_slope(value):
    return (
        0.5 * (1.0 + jax.scipy.special.erf(value * INV_ROOT_TWO))
        + value * jnp.exp(-0.5 * value * value) * INV_ROOT_TAU
    )


def combine_terms(received, flat_owner, part_rows, row_blocks, tile):
    selector = (flat_owner[:, None] == jnp.arange(row_blocks, dtype=jnp.int32)[None, :]).astype(
        jnp.float32
    )
    stacked = received.reshape(part_rows, flat_owner.shape[0], tile)
    summed = jnp.einsum("nsl,sr->nrl", stacked, selector, precision=lax.Precision.HIGHEST)
    return summed.reshape(part_rows, row_blocks * tile).astype(jnp.bfloat16)


def per_device(inputs, grad_out, w_up, w_down, up_rows, slot_counts, keep_mask):
    tok_dev, width_local = inputs.shape
    col_local, slots, tile, _unused = w_up.shape
    parts = lax.axis_size("tp")
    blocks = lax.axis_size("blk")
    width = width_local * parts
    row_blocks = width // tile
    part_rows = tok_dev // parts
    held = part_rows * blocks
    span = col_local * slots
    live = jnp.arange(slots, dtype=jnp.int32)[None, :] < slot_counts[:, None]
    live_tiles = live[:, :, None, None]
    up_live = jnp.where(live_tiles, w_up, jnp.zeros((), jnp.bfloat16))
    down_live = jnp.where(live_tiles, w_down, jnp.zeros((), jnp.bfloat16))
    owner_rows = lax.all_gather(up_rows, "blk", axis=0, tiled=True)
    flat_owner = owner_rows.reshape(-1)

    def select_tiles(rows_full):
        blocked = rows_full.reshape(part_rows, row_blocks, tile)
        return jnp.take(blocked, flat_owner, axis=1).reshape(part_rows, blocks, span * tile)

    def as_tiles(received):
        return received.reshape(held, col_local, slots, tile)

    def combine(received):
        return combine_terms(received, flat_owner, part_rows, row_blocks, tile)

    in_rows, out_rows = (
        lax.all_to_all(inputs, "tp", split_axis=0, concat_axis=1, tiled=True),
        lax.all_to_all(grad_out, "tp", split_axis=0, concat_axis=1, tiled=True),
    )
    recv_in, recv_out = (
        lax.all_to_all(select_tiles(in_rows), "blk", split_axis=1, concat_axis=0, tiled=True),
        lax.all_to_all(select_tiles(out_rows), "blk", split_axis=1, concat_axis=0, tiled=True),
    )
    input_tiles = as_tiles(recv_in)
    cotangent_tiles = as_tiles(recv_out)
    word_count = keep_mask.shape[1]
    words = keep_mask.reshape(blocks, parts, part_rows, word_count)
    mine = lax.dynamic_index_in_dim(words, lax.axis_index("tp"), 1, keepdims=False).reshape(
        held, word_count
    )
    columns = jnp.arange(col_local * tile, dtype=jnp.int32)
    picked = jnp.take(mine, columns // 16, axis=1)
    keep = jnp.bitwise_and(jnp.right_shift(picked, columns % 16), 1)
    scale = keep.astype(jnp.float32) * KEEP_SCALE
    pre = jnp.einsum(
        "nckp,ckpj->ncj", input_tiles, up_live, preferred_element_type=jnp.float32
    ).reshape(held, col_local * tile)
    hidden = (gelu_value(pre) * scale).astype(jnp.bfloat16)
    hidden_blocks = hidden.reshape(held, col_local, tile)
    out_part = jnp.einsum(
        "ncj,ckjl->nckl", hidden_blocks, down_live, preferred_element_type=jnp.float32
    ).reshape(held, span * tile)
    grad_hidden = jnp.einsum(
        "nckl,ckjl->ncj", cotangent_tiles, down_live, preferred_element_type=jnp.float32
    ).reshape(held, col_local * tile)
    grad_pre = (grad_hidden * scale * gelu_slope(pre)).astype(jnp.bfloat16)
    grad_blocks = grad_pre.reshape(held, col_local, tile)
    in_part = jnp.einsum(
        "ncj,ckpj->nckp", grad_blocks, up_live, preferred_element_type=jnp.float32
    ).reshape(held, span * tile)
    out_recv, in_recv = (
        lax.all_to_all(out_part, "blk", split_axis=0, concat_axis=1, tiled=True),
        lax.all_to_all(in_part, "blk", split_axis=0, concat_axis=1, tiled=True),
    )
    outputs, grad_in = (
        lax.all_to_all(combine(out_recv), "tp", split_axis=1, concat_axis=0, tiled=True),
        lax.all_to_all(combine(in_recv), "tp", split_axis=1, concat_axis=0, tiled=True),
    )
    up_sum = jnp.einsum(
        "nckp,ncj->ckpj", input_tiles, grad_blocks, preferred_element_type=jnp.float32
    )
    down_sum = jnp.einsum(
        "ncj,nckl->ckjl", hidden_blocks, cotangent_tiles, preferred_element_type=jnp.float32
    )
    up_share, down_share = (
        lax.psum_scatter(up_sum, "tp", scatter_dimension=2, tiled=True),
        lax.psum_scatter(down_sum, "tp", scatter_dimension=2, tiled=True),
    )
    grad_up = jnp.where(live_tiles, up_share, 0.0).astype(jnp.bfloat16)
    grad_down = jnp.where(live_tiles, down_share, 0.0).astype(jnp.bfloat16)
    return (outputs, grad_in, grad_up, grad_down)


def solution(mesh):
    return jax.shard_map(
        per_device,
        mesh=mesh,
        in_specs=(
            P("blk", "tp"),
            P("blk", "tp"),
            P("blk", None, None, None),
            P("blk", None, None, None),
            P("blk", None),
            P("blk"),
            P(None, "blk"),
        ),
        out_specs=(
            P("blk", "tp"),
            P("blk", "tp"),
            P("blk", None, "tp", None),
            P("blk", None, "tp", None),
        ),
        check_vma=False,
    )
```

profile of v0, /device:TPU:10, one launch (start us, length us, event | category | flops | bytes accessed | tf_op | source)
XLA Modules:
  0.0 286.7 jit_solution(3485483218817559302)
XLA Ops:
  7.2 3.6 %all-to-all-start = ((bf16[2,64,4096]{2,1,0:T(8,128)(2,1)}), bf16[2,64,4096]{2,1,0:T(8,128)(2,1)S(1)}, u32[]{:S(2)}, u32[]{:S(2)}) async-start(bf16[2,64,4096]{2,1,0:T(8,128)(2,1)} %bitcast.103), calls=%async_computation | async-start | bytes 2097152 | tf_op jit(solution)/shard_map/all_to_all | solution.py:59
  10.8 15.2 %all-gather = s32[16,2,2]{2,1,0:T(2,128)S(1)} all-gather(s32[1,2,2]{2,1,0:T(2,128)S(1)} %bitcast.105), channel_id=1, replica_groups=mesh['blk'=16,'tp'=2] {'blk'}, dimensions={0}, use_global_device_ids=true | all-gather | bytes 272 | tf_op jit(solution)/shard_map/all_gather | solution.py:45
  26.1 3.6 %all-to-all-start.4 = ((bf16[2,64,4096]{2,1,0:T(8,128)(2,1)}), bf16[2,64,4096]{2,1,0:T(8,128)(2,1)S(1)}, u32[]{:S(2)}, u32[]{:S(2)}) async-start(bf16[2,64,4096]{2,1,0:T(8,128)(2,1)} %bitcast.20), calls=%async_computation.4 | async-start | bytes 2097152 | tf_op jit(solution)/shard_map/all_to_all | solution.py:60
  32.3 11.9 %all-to-all-done.4 = bf16[2,64,4096]{2,1,0:T(8,128)(2,1)S(1)} async-done(((bf16[2,64,4096]{2,1,0:T(8,128)(2,1)}), bf16[2,64,4096]{2,1,0:T(8,128)(2,1)S(1)}, u32[]{:S(2)}, u32[]{:S(2)}) %all-to-all-start.4) | async-done | bytes 1048608 | tf_op jit(solution)/shard_map/all_to_all | solution.py:60
  53.6 10.4 %all-to-all-start.5 = ((bf16[64,16,512]{2,0,1:T(8,128)(2,1)}), bf16[64,16,512]{2,0,1:T(8,128)(2,1)S(1)}, u32[]{:S(2)}, u32[]{:S(2)}) async-start(bf16[64,16,512]{2,0,1:T(8,128)(2,1)} %copy.66), calls=%async_computation.5 | async-start | bytes 2097152 | tf_op jit(solution)/shard_map/all_to_all | solution.py:64
  66.9 21.7 %all-to-all-done.5 = bf16[64,16,512]{2,0,1:T(8,128)(2,1)S(1)} async-done(((bf16[64,16,512]{2,0,1:T(8,128)(2,1)}), bf16[64,16,512]{2,0,1:T(8,128)(2,1)S(1)}, u32[]{:S(2)}, u32[]{:S(2)}) %all-to-all-start.5) | async-done | bytes 1048608 | tf_op jit(solution)/shard_map/all_to_all | solution.py:64
  88.6 5.1 %all-to-all-start.1 = ((bf16[64,16,512]{2,0,1:T(8,128)(2,1)}), bf16[64,16,512]{2,0,1:T(8,128)(2,1)S(1)}, u32[]{:S(2)}, u32[]{:S(2)}) async-start(bf16[64,16,512]{2,0,1:T(8,128)(2,1)} %copy.54), calls=%async_computation.1 | async-start | bytes 2097152 | tf_op jit(solution)/shard_map/all_to_all | solution.py:63
  96.6 3.7 %copy.74 = bf16[1024,2,2,128]{0,3,2,1:T(8,128)(2,1)} copy(bf16[1024,2,2,128]{3,2,1,0:T(2,128)(2,1)} %reshape.193) | data formatting | bytes 2097152 | tf_op jit(solution)/shard_map/reshape | solution.py:53
  100.3 17.9 %all-to-all-done.1 = bf16[64,16,512]{2,0,1:T(8,128)(2,1)S(1)} async-done(((bf16[64,16,512]{2,0,1:T(8,128)(2,1)}), bf16[64,16,512]{2,0,1:T(8,128)(2,1)S(1)}, u32[]{:S(2)}, u32[]{:S(2)}) %all-to-all-start.1) | async-done | bytes 1048608 | tf_op jit(solution)/shard_map/all_to_all | solution.py:63
  119.3 2.5 copy.72
  126.6 3.1 %copy.69 = f32[1024,2,2,128]{3,2,1,0:T(2,128)S(1)} copy(f32[1024,2,2,128]{0,3,2,1:T(8,128)} %convolution_bitcast_fusion) | data formatting | bytes 4194304 | tf_op jit(solution)/shard_map/ncj,ckpj->nckp/transpose | solution.py:90
  129.7 2.7 all_to_all.112
  132.4 5.1 %all-to-all-start.6 = ((f32[16,64,512]{2,1,0:T(8,128)}), f32[16,64,512]{2,1,0:T(8,128)S(1)}, u32[]{:S(2)}, u32[]{:S(2)}) async-start(f32[16,64,512]{2,1,0:T(8,128)} %all_to_all.112), calls=%async_computation.6 | async-start | bytes 4194304 | tf_op jit(solution)/shard_map/all_to_all | solution.py:95
  137.5 2.0 fusion.10
  140.3 1.9 convolution_bitcast_fusion.1
  142.2 4.1 %copy.60 = f32[1024,2,2,128]{3,2,1,0:T(2,128)} copy(f32[1024,2,2,128]{0,3,2,1:T(8,128)} %convolution_bitcast_fusion.1) | data formatting | bytes 4194304 | tf_op jit(solution)/shard_map/ncj,ckjl->nckl/transpose | solution.py:82
  146.3 3.9 %all_to_all.100 = f32[16,64,512]{2,1,0:T(8,128)} reshape(f32[1024,2,2,128]{3,2,1,0:T(2,128)} %copy.60) | data formatting | bytes 4194304 | tf_op jit(solution)/shard_map/all_to_all | solution.py:94
  150.2 34.4 %all-to-all-done.6 = f32[16,64,512]{2,1,0:T(8,128)S(1)} async-done(((f32[16,64,512]{2,1,0:T(8,128)}), f32[16,64,512]{2,1,0:T(8,128)S(1)}, u32[]{:S(2)}, u32[]{:S(2)}) %all-to-all-start.6) | async-done | bytes 2097184 | tf_op jit(solution)/shard_map/all_to_all | solution.py:95
  185.9 5.1 %all-to-all-start.2 = ((f32[16,64,512]{2,1,0:T(8,128)}), f32[16,64,512]{2,1,0:T(8,128)S(1)}, u32[]{:S(2)}, u32[]{:S(2)}) async-start(f32[16,64,512]{2,1,0:T(8,128)} %all_to_all.100), calls=%async_computation.2 | async-start | bytes 4194304 | tf_op jit(solution)/shard_map/all_to_all | solution.py:94
  191.0 2.2 fusion.26
  193.3 4.2 %copy.70 = f32[64,16,512]{2,1,0:T(8,128)} copy(f32[64,16,512]{2,0,1:T(8,128)} %bitcast.95) | data formatting | bytes 4194304 | tf_op jit(solution)/shard_map/all_to_all | solution.py:95
  197.4 2.6 reshape.194
  200.1 2.8 fusion.1
  204.0 2.8 copy.71
  206.9 31.3 %all-to-all-done.2 = f32[16,64,512]{2,1,0:T(8,128)S(1)} async-done(((f32[16,64,512]{2,1,0:T(8,128)}), f32[16,64,512]{2,1,0:T(8,128)S(1)}, u32[]{:S(2)}, u32[]{:S(2)}) %all-to-all-start.2) | async-done | bytes 2097184 | tf_op jit(solution)/shard_map/all_to_all | solution.py:94
  238.1 4.4 %all-to-all-start.7 = ((bf16[64,2,4096]{2,0,1:T(8,128)(2,1)}), bf16[64,2,4096]{2,0,1:T(8,128)(2,1)}, u32[]{:S(2)}, u32[]{:S(2)}) async-start(bf16[64,2,4096]{2,0,1:T(8,128)(2,1)} %copy.71), calls=%async_computation.7 | async-start | bytes 2097152 | tf_op jit(solution)/shard_map/all_to_all | solution.py:99
  242.8 2.4 convolution_bitcast_fusion.4
  245.3 2.6 copy.61
  252.6 7.3 %all-to-all-done.7 = bf16[64,2,4096]{2,0,1:T(8,128)(2,1)} async-done(((bf16[64,2,4096]{2,0,1:T(8,128)(2,1)}), bf16[64,2,4096]{2,0,1:T(8,128)(2,1)}, u32[]{:S(2)}, u32[]{:S(2)}) %all-to-all-start.7) | async-done | bytes 1048608 | tf_op jit(solution)/shard_map/all_to_all | solution.py:99
  259.9 3.6 %all-to-all-start.3 = ((bf16[64,2,4096]{2,0,1:T(8,128)(2,1)}), bf16[64,2,4096]{2,0,1:T(8,128)(2,1)S(1)}, u32[]{:S(2)}, u32[]{:S(2)}) async-start(bf16[64,2,4096]{2,0,1:T(8,128)(2,1)} %copy.62), calls=%async_computation.3 | async-start | bytes 2097152 | tf_op jit(solution)/shard_map/all_to_all | solution.py:98
  265.3 11.3 %all-to-all-done.3 = bf16[64,2,4096]{2,0,1:T(8,128)(2,1)S(1)} async-done(((bf16[64,2,4096]{2,0,1:T(8,128)(2,1)}), bf16[64,2,4096]{2,0,1:T(8,128)(2,1)S(1)}, u32[]{:S(2)}, u32[]{:S(2)}) %all-to-all-start.3) | async-done | bytes 1048608 | tf_op jit(solution)/shard_map/all_to_all | solution.py:98
  277.6 2.3 copy.98
  (75 shorter events, 34.6 us)
Async XLA Ops:
  7.2 3.6 %copy-start.12 = (s32[2,2]{1,0:T(2,128)S(1)}, s32[2,2]{1,0:T(2,128)}, u32[]{:S(2)}) copy-start(s32[2,2]{1,0:T(2,128)} %param.13) | copy-start | bytes 52
  7.2 18.9 %all-to-all-start = ((bf16[2,64,4096]{2,1,0:T(8,128)(2,1)}), bf16[2,64,4096]{2,1,0:T(8,128)(2,1)S(1)}, u32[]{:S(2)}, u32[]{:S(2)}) async-start(bf16[2,64,4096]{2,1,0:T(8,128)(2,1)} %bitcast.103), calls=%async_computation | async-start | bytes 2097152 | tf_op jit(solution)/shard_map/all_to_all | solution.py:59
  26.1 18.2 %all-to-all-start.4 = ((bf16[2,64,4096]{2,1,0:T(8,128)(2,1)}), bf16[2,64,4096]{2,1,0:T(8,128)(2,1)S(1)}, u32[]{:S(2)}, u32[]{:S(2)}) async-start(bf16[2,64,4096]{2,1,0:T(8,128)(2,1)} %bitcast.20), calls=%async_computation.4 | async-start | bytes 2097152 | tf_op jit(solution)/shard_map/all_to_all | solution.py:60
  53.6 35.0 %all-to-all-start.5 = ((bf16[64,16,512]{2,0,1:T(8,128)(2,1)}), bf16[64,16,512]{2,0,1:T(8,128)(2,1)S(1)}, u32[]{:S(2)}, u32[]{:S(2)}) async-start(bf16[64,16,512]{2,0,1:T(8,128)(2,1)} %copy.66), calls=%async_computation.5 | async-start | bytes 2097152 | tf_op jit(solution)/shard_map/all_to_all | solution.py:64
  65.3 28.3 %copy-start.10 = (s32[2048,16]{0,1:T(8,128)S(1)}, s32[2048,16]{0,1:T(8,128)}, u32[]{:S(2)}) copy-start(s32[2048,16]{0,1:T(8,128)} %param.15) | copy-start | bytes 393220
  88.6 5.4 %copy-start.5 = (bf16[64,16,512]{2,0,1:T(8,128)(2,1)}, bf16[64,16,512]{2,0,1:T(8,128)(2,1)S(1)}, u32[]{:S(2)}) copy-start(bf16[64,16,512]{2,0,1:T(8,128)(2,1)S(1)} %all-to-all-done.5) | copy-start | bytes 3145732
  88.6 29.7 %all-to-all-start.1 = ((bf16[64,16,512]{2,0,1:T(8,128)(2,1)}), bf16[64,16,512]{2,0,1:T(8,128)(2,1)S(1)}, u32[]{:S(2)}, u32[]{:S(2)}) async-start(bf16[64,16,512]{2,0,1:T(8,128)(2,1)} %copy.54), calls=%async_computation.1 | async-start | bytes 2097152 | tf_op jit(solution)/shard_map/all_to_all | solution.py:63
  94.1 1.1 copy-start.13
  94.1 1.2 copy-start.6
  95.2 27.0 %copy-start.3 = (s32[256,1024]{1,0:T(8,128)}, s32[256,1024]{1,0:T(8,128)S(1)}, u32[]{:S(2)}) copy-start(s32[256,1024]{1,0:T(8,128)S(1)} %gather_fusion) | copy-start | bytes 3145732
  118.2 3.6 %copy-start.9 = (bf16[2,2,128,128]{3,2,1,0:T(8,128)(2,1)S(1)}, bf16[2,2,128,128]{3,2,1,0:T(8,128)(2,1)}, u32[]{:S(2)}) copy-start(bf16[2,2,128,128]{3,2,1,0:T(8,128)(2,1)} %param.11) | copy-start | bytes 393220
  119.3 3.0 %copy-start.11 = (bf16[2,2,128,128]{3,2,1,0:T(8,128)(2,1)S(1)}, bf16[2,2,128,128]{3,2,1,0:T(8,128)(2,1)}, u32[]{:S(2)}) copy-start(bf16[2,2,128,128]{3,2,1,0:T(8,128)(2,1)} %param.12) | copy-start | bytes 393220
  121.8 1.2 copy-start.4
  122.3 1.6 copy-start.7
  123.9 0.8 copy-start.8
  132.4 52.2 %all-to-all-start.6 = ((f32[16,64,512]{2,1,0:T(8,128)}), f32[16,64,512]{2,1,0:T(8,128)S(1)}, u32[]{:S(2)}, u32[]{:S(2)}) async-start(f32[16,64,512]{2,1,0:T(8,128)} %all_to_all.112), calls=%async_computation.6 | async-start | bytes 4194304 | tf_op jit(solution)/shard_map/all_to_all | solution.py:95
  139.4 0.8 copy-start.1
  184.6 1.3 copy-start
  185.9 52.2 %all-to-all-start.2 = ((f32[16,64,512]{2,1,0:T(8,128)}), f32[16,64,512]{2,1,0:T(8,128)S(1)}, u32[]{:S(2)}, u32[]{:S(2)}) async-start(f32[16,64,512]{2,1,0:T(8,128)} %all_to_all.100), calls=%async_computation.2 | async-start | bytes 4194304 | tf_op jit(solution)/shard_map/all_to_all | solution.py:94
  191.0 72.5 %reduce-scatter.3.cloned.1.call-start = ((), (), s32[]{:S(2)}) async-start(), calls=%async_computation.10 | async-start | bytes 393216 | tf_op jit(solution)/shard_map/reduce_scatter | solution.py:108
  204.0 38.8 %copy-start.2 = (bf16[1024,2,128,1]{0,2,3,1:T(8,128)(2,1)S(1)}, bf16[1024,2,128,1]{0,2,3,1:T(8,128)(2,1)}, u32[]{:S(2)}) copy-start(bf16[1024,2,128,1]{0,2,3,1:T(8,128)(2,1)} %copy-done.1) | copy-start | bytes 1572868
  238.1 21.8 %all-to-all-start.7 = ((bf16[64,2,4096]{2,0,1:T(8,128)(2,1)}), bf16[64,2,4096]{2,0,1:T(8,128)(2,1)}, u32[]{:S(2)}, u32[]{:S(2)}) async-start(bf16[64,2,4096]{2,0,1:T(8,128)(2,1)} %copy.71), calls=%async_computation.7 | async-start | bytes 2097152 | tf_op jit(solution)/shard_map/all_to_all | solution.py:99
  242.6 21.0 %reduce-scatter.5.cloned.1.call-start = ((), (), s32[]{:S(2)}) async-start(), calls=%async_computation.11 | async-start | bytes 393216 | tf_op jit(solution)/shard_map/reduce_scatter | solution.py:109
  259.9 16.7 %all-to-all-start.3 = ((bf16[64,2,4096]{2,0,1:T(8,128)(2,1)}), bf16[64,2,4096]{2,0,1:T(8,128)(2,1)S(1)}, u32[]{:S(2)}, u32[]{:S(2)}) async-start(bf16[64,2,4096]{2,0,1:T(8,128)(2,1)} %copy.62), calls=%async_computation.3 | async-start | bytes 2097152 | tf_op jit(solution)/shard_map/all_to_all | solution.py:98
Sparse Core Ops, SparseCore 0:
  194.0 11.7 reduce-scatter.2
  245.6 14.8 reduce-scatter.4
where the time goes:
time: 288 us; the launch traced here: 287 us
  waiting for transfers between devices  136 us (47%)
  local copies, waits for them, and re-layouts  62.2 us (22%)
  starting transfers between devices  41.1 us (14%)
  blocking collectives  15.2 us (5%)
  between operations  14.5 us (5%)
  matrix products  13.7 us (5%)
  other arithmetic  4.05 us (1%)
    all_to_all x1, waiting for transfers between devices, per_device(): lax.all_to_all(in_part, 'blk', split_axis=0, concat_axis=1, tiled=True)  34.4 us
    all_to_all x1, waiting for transfers between devices, per_device(): lax.all_to_all(out_part, 'blk', split_axis=0, concat_axis=1, tiled=True)  31.3 us
    all_to_all x1, waiting for transfers between devices, per_device(): lax.all_to_all(select_tiles(out_rows), 'blk', split_axis=1, concat_axis=0...  21.7 us
    all_to_all x1, waiting for transfers between devices, per_device(): lax.all_to_all(select_tiles(in_rows), 'blk', split_axis=1, concat_axis=0,...  17.9 us
    all_gather x1, blocking collectives, per_device(): owner_rows = lax.all_gather(up_rows, 'blk', axis=0, tiled=True)  15.2 us
    all_to_all x1, waiting for transfers between devices, per_device(): lax.all_to_all(grad_out, 'tp', split_axis=0, concat_axis=1, tiled=True)  11.9 us
    all_to_all x1, waiting for transfers between devices, per_device(): lax.all_to_all(combine(out_recv), 'tp', split_axis=1, concat_axis=0, tile...  11.3 us
    all_to_all x1, starting transfers between devices, per_device(): lax.all_to_all(select_tiles(out_rows), 'blk', split_axis=1, concat_axis=0...  10.4 us
  transfers between devices with their start and end apart: 10, of which 7 were waited for; matrix products, arithmetic and copies ran while one was open for 17% of the time, Pallas kernels for 0%

commit v1 on v0

--- a/solution.py
+++ b/solution.py
@@ -6,6 +6,13 @@
 INV_ROOT_TWO = 0.7071067811865476
 INV_ROOT_TAU = 0.3989422804014327
 KEEP_SCALE = 1.25
+
+
+def swap_blocks(block, name, split, join):
+    size = lax.axis_size(name)
+    tiles = jnp.stack(jnp.split(block, size, axis=split), axis=0)
+    tiles = lax.all_to_all(tiles, name, split_axis=0, concat_axis=0)
+    return jnp.concatenate(tiles, axis=join)
 
 
 def gelu_value(value):
@@ -61,7 +68,7 @@
     )
     recv_in, recv_out = (
         lax.all_to_all(select_tiles(in_rows), "blk", split_axis=1, concat_axis=0, tiled=True),
-        lax.all_to_all(select_tiles(out_rows), "blk", split_axis=1, concat_axis=0, tiled=True),
+        swap_blocks(select_tiles(out_rows), "blk", 1, 0),
     )
     input_tiles = as_tiles(recv_in)
     cotangent_tiles = as_tiles(recv_out)

time: 288 us -> 299 us (1.038)
  local copies, waits for them, and re-layouts: 62.2 us -> 72.8 us
    unnamed x30 -> x45, local copies, waits for them, and re-layouts: 7.06 us -> 16.7 us
    another operation x0 -> x3, local copies, waits for them, and re-layouts: none -> 5.53 us  [the longest x2 4.89 us: as_tiles(): return received.reshape(held, col_local, slots, tile)]
    reshape x4 -> x2, local copies, waits for them, and re-layouts: 8.48 us -> 3.58 us  [as_tiles(): return received.reshape(held, col_local, slots, tile)]
  transfers between devices with their start and end apart: 10 -> 10, of which waited for: 7 -> 7; matrix products, arithmetic and copies ran while one was open for 17% -> 16% of each run, Pallas kernels for 0% -> 0%
where the time goes in v1:
time: 299 us; the launch traced here: 297 us
  waiting for transfers between devices  136 us (45%)
  local copies, waits for them, and re-layouts  72.8 us (24%)
  starting transfers between devices  41.1 us (14%)
  blocking collectives  15.2 us (5%)
  between operations  14.5 us (5%)
  matrix products  13.7 us (5%)
  other arithmetic  4.05 us (1%)
    all_to_all x1, waiting for transfers between devices, per_device(): lax.all_to_all(in_part, 'blk', split_axis=0, concat_axis=1, tiled=True)  34.4 us
    all_to_all x1, waiting for transfers between devices, per_device(): lax.all_to_all(out_part, 'blk', split_axis=0, concat_axis=1, tiled=True)  31.3 us
    all_to_all x1, waiting for transfers between devices, swap_blocks(): tiles = lax.all_to_all(tiles, name, split_axis=0, concat_axis=0)  21.7 us
    all_to_all x1, waiting for transfers between devices, per_device(): lax.all_to_all(select_tiles(in_rows), 'blk', split_axis=1, concat_axis=0,...  18 us
    unnamed x45, local copies, waits for them, and re-layouts  16.7 us
    all_gather x1, blocking collectives, per_device(): owner_rows = lax.all_gather(up_rows, 'blk', axis=0, tiled=True)  15.2 us
    all_to_all x1, waiting for transfers between devices, per_device(): lax.all_to_all(grad_out, 'tp', split_axis=0, concat_axis=1, tiled=True)  11.9 us
    all_to_all x1, waiting for transfers between devices, per_device(): lax.all_to_all(combine(out_recv), 'tp', split_axis=1, concat_axis=0, tile...  11.3 us
  transfers between devices with their start and end apart: 10, of which 7 were waited for; matrix products, arithmetic and copies ran while one was open for 16% of the time, Pallas kernels for 0%

profile of v1, /device:TPU:10, one launch (start us, length us, event | category | flops | bytes accessed | tf_op | source)
XLA Modules:
  0.0 297.2 jit_solution(13394984744151523534)
XLA Ops:
  7.2 3.6 %all-to-all-start = ((bf16[2,64,4096]{2,1,0:T(8,128)(2,1)}), bf16[2,64,4096]{2,1,0:T(8,128)(2,1)S(1)}, u32[]{:S(2)}, u32[]{:S(2)}) async-start(bf16[2,64,4096]{2,1,0:T(8,128)(2,1)} %bitcast.131), calls=%async_computation | async-start | bytes 2097152 | tf_op jit(solution)/shard_map/all_to_all | solution.py:66
  10.8 15.2 %all-gather = s32[16,2,2]{2,1,0:T(2,128)S(1)} all-gather(s32[1,2,2]{2,1,0:T(2,128)S(1)} %bitcast.133), channel_id=1, replica_groups=mesh['blk'=16,'tp'=2] {'blk'}, dimensions={0}, use_global_device_ids=true | all-gather | bytes 272 | tf_op jit(solution)/shard_map/all_gather | solution.py:52
  26.1 3.6 %all-to-all-start.4 = ((bf16[2,64,4096]{2,1,0:T(8,128)(2,1)}), bf16[2,64,4096]{2,1,0:T(8,128)(2,1)S(1)}, u32[]{:S(2)}, u32[]{:S(2)}) async-start(bf16[2,64,4096]{2,1,0:T(8,128)(2,1)} %bitcast.20), calls=%async_computation.4 | async-start | bytes 2097152 | tf_op jit(solution)/shard_map/all_to_all | solution.py:67
  32.4 11.9 %all-to-all-done.4 = bf16[2,64,4096]{2,1,0:T(8,128)(2,1)S(1)} async-done(((bf16[2,64,4096]{2,1,0:T(8,128)(2,1)}), bf16[2,64,4096]{2,1,0:T(8,128)(2,1)S(1)}, u32[]{:S(2)}, u32[]{:S(2)}) %all-to-all-start.4) | async-done | bytes 1048608 | tf_op jit(solution)/shard_map/all_to_all | solution.py:67
  47.0 1.9 copy.558
  64.1 10.4 %all-to-all-start.5 = ((bf16[16,64,1,512]{3,1,2,0:T(8,128)(2,1)}), bf16[16,64,1,512]{3,1,2,0:T(8,128)(2,1)S(1)}, u32[]{:S(2)}, u32[]{:S(2)}) async-start(bf16[16,64,1,512]{3,1,2,0:T(8,128)(2,1)} %bitcast_dynamic-update-slice_fusion), calls=%async_computation.5 | async-start | bytes 2097152 | tf_op jit(solution)/shard_map/all_to_all | solution.py:14
  77.4 21.7 %all-to-all-done.5 = bf16[16,64,1,512]{3,1,2,0:T(8,128)(2,1)S(1)} async-done(((bf16[16,64,1,512]{3,1,2,0:T(8,128)(2,1)}), bf16[16,64,1,512]{3,1,2,0:T(8,128)(2,1)S(1)}, u32[]{:S(2)}, u32[]{:S(2)}) %all-to-all-start.5) | async-done | bytes 1048608 | tf_op jit(solution)/shard_map/all_to_all | solution.py:14
  99.1 5.1 %all-to-all-start.1 = ((bf16[64,16,512]{2,0,1:T(8,128)(2,1)}), bf16[64,16,512]{2,0,1:T(8,128)(2,1)S(1)}, u32[]{:S(2)}, u32[]{:S(2)}) async-start(bf16[64,16,512]{2,0,1:T(8,128)(2,1)} %copy.548), calls=%async_computation.1 | async-start | bytes 2097152 | tf_op jit(solution)/shard_map/all_to_all | solution.py:70
  107.1 3.7 %copy.567 = bf16[1024,2,2,128]{0,3,2,1:T(8,128)(2,1)} copy(bf16[1024,2,2,128]{3,2,1,0:T(2,128)(2,1)} %reshape_reshape.3) | data formatting | bytes 2097152 | tf_op jit(solution)/shard_map/reshape;reshape | solution.py:60
  110.8 18.0 %all-to-all-done.1 = bf16[64,16,512]{2,0,1:T(8,128)(2,1)S(1)} async-done(((bf16[64,16,512]{2,0,1:T(8,128)(2,1)}), bf16[64,16,512]{2,0,1:T(8,128)(2,1)S(1)}, u32[]{:S(2)}, u32[]{:S(2)}) %all-to-all-start.1) | async-done | bytes 1048608 | tf_op jit(solution)/shard_map/all_to_all | solution.py:70
  129.9 2.5 copy.565
  137.1 3.1 %copy.562 = f32[1024,2,2,128]{3,2,1,0:T(2,128)S(1)} copy(f32[1024,2,2,128]{0,3,2,1:T(8,128)} %convolution_bitcast_fusion) | data formatting | bytes 4194304 | tf_op jit(solution)/shard_map/ncj,ckpj->nckp/transpose | solution.py:97
  140.2 2.7 all_to_all.102
  142.9 5.1 %all-to-all-start.6 = ((f32[16,64,512]{2,1,0:T(8,128)}), f32[16,64,512]{2,1,0:T(8,128)S(1)}, u32[]{:S(2)}, u32[]{:S(2)}) async-start(f32[16,64,512]{2,1,0:T(8,128)} %all_to_all.102), calls=%async_computation.6 | async-start | bytes 4194304 | tf_op jit(solution)/shard_map/all_to_all | solution.py:102
  148.0 2.0 fusion.10
  152.7 4.1 %copy.554 = f32[1024,2,2,128]{3,2,1,0:T(2,128)} copy(f32[1024,2,2,128]{0,3,2,1:T(8,128)} %convolution_bitcast_fusion.1) | data formatting | bytes 4194304 | tf_op jit(solution)/shard_map/ncj,ckjl->nckl/transpose | solution.py:89
  156.9 3.9 %all_to_all.92 = f32[16,64,512]{2,1,0:T(8,128)} reshape(f32[1024,2,2,128]{3,2,1,0:T(2,128)} %copy.554) | data formatting | bytes 4194304 | tf_op jit(solution)/shard_map/all_to_all | solution.py:101
  160.7 34.4 %all-to-all-done.6 = f32[16,64,512]{2,1,0:T(8,128)S(1)} async-done(((f32[16,64,512]{2,1,0:T(8,128)}), f32[16,64,512]{2,1,0:T(8,128)S(1)}, u32[]{:S(2)}, u32[]{:S(2)}) %all-to-all-start.6) | async-done | bytes 2097184 | tf_op jit(solution)/shard_map/all_to_all | solution.py:102
  196.5 5.1 %all-to-all-start.2 = ((f32[16,64,512]{2,1,0:T(8,128)}), f32[16,64,512]{2,1,0:T(8,128)S(1)}, u32[]{:S(2)}, u32[]{:S(2)}) async-start(f32[16,64,512]{2,1,0:T(8,128)} %all_to_all.92), calls=%async_computation.2 | async-start | bytes 4194304 | tf_op jit(solution)/shard_map/all_to_all | solution.py:101
  201.6 2.2 fusion.27
  203.8 4.2 %copy.563 = f32[64,16,512]{2,1,0:T(8,128)} copy(f32[64,16,512]{2,0,1:T(8,128)} %bitcast.124) | data formatting | bytes 4194304 | tf_op jit(solution)/shard_map/all_to_all | solution.py:102
  208.0 2.6 reshape.189
  210.6 2.8 fusion.1
  214.6 2.8 copy.564
  217.4 31.3 %all-to-all-done.2 = f32[16,64,512]{2,1,0:T(8,128)S(1)} async-done(((f32[16,64,512]{2,1,0:T(8,128)}), f32[16,64,512]{2,1,0:T(8,128)S(1)}, u32[]{:S(2)}, u32[]{:S(2)}) %all-to-all-start.2) | async-done | bytes 2097184 | tf_op jit(solution)/shard_map/all_to_all | solution.py:101
  248.7 4.4 %all-to-all-start.7 = ((bf16[64,2,4096]{2,0,1:T(8,128)(2,1)}), bf16[64,2,4096]{2,0,1:T(8,128)(2,1)}, u32[]{:S(2)}, u32[]{:S(2)}) async-start(bf16[64,2,4096]{2,0,1:T(8,128)(2,1)} %copy.564), calls=%async_computation.7 | async-start | bytes 2097152 | tf_op jit(solution)/shard_map/all_to_all | solution.py:106
  253.4 2.4 convolution_bitcast_fusion.4
  255.8 2.6 copy.555
  263.2 7.3 %all-to-all-done.7 = bf16[64,2,4096]{2,0,1:T(8,128)(2,1)} async-done(((bf16[64,2,4096]{2,0,1:T(8,128)(2,1)}), bf16[64,2,4096]{2,0,1:T(8,128)(2,1)}, u32[]{:S(2)}, u32[]{:S(2)}) %all-to-all-start.7) | async-done | bytes 1048608 | tf_op jit(solution)/shard_map/all_to_all | solution.py:106
  270.4 3.6 %all-to-all-start.3 = ((bf16[64,2,4096]{2,0,1:T(8,128)(2,1)}), bf16[64,2,4096]{2,0,1:T(8,128)(2,1)S(1)}, u32[]{:S(2)}, u32[]{:S(2)}) async-start(bf16[64,2,4096]{2,0,1:T(8,128)(2,1)} %copy.556), calls=%async_computation.3 | async-start | bytes 2097152 | tf_op jit(solution)/shard_map/all_to_all | solution.py:105
  275.8 11.3 %all-to-all-done.3 = bf16[64,2,4096]{2,0,1:T(8,128)(2,1)S(1)} async-done(((bf16[64,2,4096]{2,0,1:T(8,128)(2,1)}), bf16[64,2,4096]{2,0,1:T(8,128)(2,1)S(1)}, u32[]{:S(2)}, u32[]{:S(2)}) %all-to-all-start.3) | async-done | bytes 1048608 | tf_op jit(solution)/shard_map/all_to_all | solution.py:105
  288.1 2.3 copy.638
  (90 shorter events, 45.1 us)
Async XLA Ops:
  7.2 3.6 %copy-start.12 = (s32[2,2]{1,0:T(2,128)S(1)}, s32[2,2]{1,0:T(2,128)}, u32[]{:S(2)}) copy-start(s32[2,2]{1,0:T(2,128)} %param.13) | copy-start | bytes 52
  7.2 18.9 %all-to-all-start = ((bf16[2,64,4096]{2,1,0:T(8,128)(2,1)}), bf16[2,64,4096]{2,1,0:T(8,128)(2,1)S(1)}, u32[]{:S(2)}, u32[]{:S(2)}) async-start(bf16[2,64,4096]{2,1,0:T(8,128)(2,1)} %bitcast.131), calls=%async_computation | async-start | bytes 2097152 | tf_op jit(solution)/shard_map/all_to_all | solution.py:66
  26.1 18.2 %all-to-all-start.4 = ((bf16[2,64,4096]{2,1,0:T(8,128)(2,1)}), bf16[2,64,4096]{2,1,0:T(8,128)(2,1)S(1)}, u32[]{:S(2)}, u32[]{:S(2)}) async-start(bf16[2,64,4096]{2,1,0:T(8,128)(2,1)} %bitcast.20), calls=%async_computation.4 | async-start | bytes 2097152 | tf_op jit(solution)/shard_map/all_to_all | solution.py:67
  64.1 35.0 %all-to-all-start.5 = ((bf16[16,64,1,512]{3,1,2,0:T(8,128)(2,1)}), bf16[16,64,1,512]{3,1,2,0:T(8,128)(2,1)S(1)}, u32[]{:S(2)}, u32[]{:S(2)}) async-start(bf16[16,64,1,512]{3,1,2,0:T(8,128)(2,1)} %bitcast_dynamic-update-slice_fusion), calls=%async_computation.5 | async-start | bytes 2097152 | tf_op jit(solution)/shard_map/all_to_all | solution.py:14
  75.9 28.3 %copy-start.10 = (s32[2048,16]{0,1:T(8,128)S(1)}, s32[2048,16]{0,1:T(8,128)}, u32[]{:S(2)}) copy-start(s32[2048,16]{0,1:T(8,128)} %param.15) | copy-start | bytes 393220
  99.1 5.4 %copy-start.5 = (bf16[16,64,1,512]{3,1,2,0:T(8,128)(2,1)}, bf16[16,64,1,512]{3,1,2,0:T(8,128)(2,1)S(1)}, u32[]{:S(2)}) copy-start(bf16[16,64,1,512]{3,1,2,0:T(8,128)(2,1)S(1)} %all-to-all-done.5) | copy-start | bytes 3145732
  99.1 29.7 %all-to-all-start.1 = ((bf16[64,16,512]{2,0,1:T(8,128)(2,1)}), bf16[64,16,512]{2,0,1:T(8,128)(2,1)S(1)}, u32[]{:S(2)}, u32[]{:S(2)}) async-start(bf16[64,16,512]{2,0,1:T(8,128)(2,1)} %copy.548), calls=%async_computation.1 | async-start | bytes 2097152 | tf_op jit(solution)/shard_map/all_to_all | solution.py:70
  104.7 1.1 copy-start.13
  104.7 1.2 copy-start.6
  105.7 27.1 %copy-start.3 = (s32[256,1024]{1,0:T(8,128)}, s32[256,1024]{1,0:T(8,128)S(1)}, u32[]{:S(2)}) copy-start(s32[256,1024]{1,0:T(8,128)S(1)} %gather_fusion) | copy-start | bytes 3145732
  128.8 3.6 %copy-start.9 = (bf16[2,2,128,128]{3,2,1,0:T(8,128)(2,1)S(1)}, bf16[2,2,128,128]{3,2,1,0:T(8,128)(2,1)}, u32[]{:S(2)}) copy-start(bf16[2,2,128,128]{3,2,1,0:T(8,128)(2,1)} %param.11) | copy-start | bytes 393220
  129.9 3.0 copy-start.11
  132.4 1.2 copy-start.4
  132.8 1.6 copy-start.7
  134.4 0.8 copy-start.8
  142.9 52.2 %all-to-all-start.6 = ((f32[16,64,512]{2,1,0:T(8,128)}), f32[16,64,512]{2,1,0:T(8,128)S(1)}, u32[]{:S(2)}, u32[]{:S(2)}) async-start(f32[16,64,512]{2,1,0:T(8,128)} %all_to_all.102), calls=%async_computation.6 | async-start | bytes 4194304 | tf_op jit(solution)/shard_map/all_to_all | solution.py:102
  150.0 0.8 copy-start.1
  195.2 1.3 copy-start
  196.5 52.2 %all-to-all-start.2 = ((f32[16,64,512]{2,1,0:T(8,128)}), f32[16,64,512]{2,1,0:T(8,128)S(1)}, u32[]{:S(2)}, u32[]{:S(2)}) async-start(f32[16,64,512]{2,1,0:T(8,128)} %all_to_all.92), calls=%async_computation.2 | async-start | bytes 4194304 | tf_op jit(solution)/shard_map/all_to_all | solution.py:101
  201.5 72.5 %reduce-scatter.3.cloned.1.call-start = ((), (), s32[]{:S(2)}) async-start(), calls=%async_computation.10 | async-start | bytes 393216 | tf_op jit(solution)/shard_map/reduce_scatter | solution.py:115
  214.6 38.8 %copy-start.2 = (bf16[1024,2,128,1]{0,2,3,1:T(8,128)(2,1)S(1)}, bf16[1024,2,128,1]{0,2,3,1:T(8,128)(2,1)}, u32[]{:S(2)}) copy-start(bf16[1024,2,128,1]{0,2,3,1:T(8,128)(2,1)} %copy-done.1) | copy-start | bytes 1572868
  248.7 21.8 %all-to-all-start.7 = ((bf16[64,2,4096]{2,0,1:T(8,128)(2,1)}), bf16[64,2,4096]{2,0,1:T(8,128)(2,1)}, u32[]{:S(2)}, u32[]{:S(2)}) async-start(bf16[64,2,4096]{2,0,1:T(8,128)(2,1)} %copy.564), calls=%async_computation.7 | async-start | bytes 2097152 | tf_op jit(solution)/shard_map/all_to_all | solution.py:106
  253.1 21.0 %reduce-scatter.5.cloned.1.call-start = ((), (), s32[]{:S(2)}) async-start(), calls=%async_computation.11 | async-start | bytes 393216 | tf_op jit(solution)/shard_map/reduce_scatter | solution.py:116
  270.4 16.7 %all-to-all-start.3 = ((bf16[64,2,4096]{2,0,1:T(8,128)(2,1)}), bf16[64,2,4096]{2,0,1:T(8,128)(2,1)S(1)}, u32[]{:S(2)}, u32[]{:S(2)}) async-start(bf16[64,2,4096]{2,0,1:T(8,128)(2,1)} %copy.556), calls=%async_computation.3 | async-start | bytes 2097152 | tf_op jit(solution)/shard_map/all_to_all | solution.py:105
Sparse Core Ops, SparseCore 0:
  204.6 11.7 reduce-scatter.2
  256.2 14.8 reduce-scatter.4
